TPU v7x, 32 devices: a whole 2x2x4 slice. The times are simulated.
32 devices in a mesh: groups: 2 (over x), seq: 16 (over z, y, core).
Axes of the slice: x: 2, y: 2, z: 4, core: 2. Of those that a mesh axis runs over, the one named last changes fastest.
Arguments:
- enc_input: bfloat16 [8192, 1408], P(('groups', 'seq')), parts along dimension 0, may hold values from -6 to 6
- enc_weight: bfloat16 [2816, 1536], P('seq'), may hold values from -0.109375 to 0.109375
- norm_gain: float32 [1536], replicated, may hold values from 0.5 to 1.5
- q_weight: bfloat16 [1536, 1024], replicated, may hold values from -1 to 1
- kv_weight: bfloat16 [1536, 320], replicated, may hold values from -1 to 1
- out_weight: bfloat16 [1536, 1536], replicated, may hold values from -0.15625 to 0.15625
- dec_weight: float32 [3, 1536], replicated, may hold values from -3 to 3
- track_weight: bfloat16 [192, 1536], P('seq'), may hold values from -0.15625 to 0.15625
- track_grad: bfloat16 [4096, 192], P('groups', 'seq'), parts along dimension 0, may hold values from -6 to 6
- track_index: int32 [384], P('groups'), parts along dimension 0, may hold values from 0 to 191, each once
- track_mask: int32 [384], P('groups'), parts along dimension 0, may hold values 0 or 1
Outputs:
- trunk_out: bfloat16 [4096, 1536], P(('groups', 'seq')), parts along dimension 0
- skip_grad: bfloat16 [4096, 1536], P(('groups', 'seq')), parts along dimension 0
- dec_weight_grad: float32 [6, 1536], P('groups'), parts along dimension 0
There are 2 independent parts, one for each index of `groups`. A program takes and returns all parts, laid end to end along the dimension named above; an argument that names none is the same for every part. Nothing has to cross between parts.
Inputs may be any that keep to these rules, and one draw needn't show every extreme that they name: `track_index`: names every track once.
All inputs are finite; a program needn't handle non-finite values.
Results may differ from a plain program's by a relative error of at most 0.02.
Values may be sent and summed in bfloat16 or wider, within the bound.
No kernel may reach another device: no remote copies, remote signals or barrier semaphores. Data moves between devices by JAX's collectives and lax.ppermute only.
A program may use at most 128 MiB of HBM per device.

v0:
```python
import math
import jax
import jax.numpy as jnp
from jax import lax
from jax.sharding import PartitionSpec as P

HEADS = 8
QK = 128
VDIM = 192
DILATION_SPAN = 8


def with_halo(cells, sides, width):
    for axis, dim in sides:
        count = lax.axis_size(axis)
        ends = count - 1
        head = lax.slice_in_dim(cells, 0, width, axis=dim)
        tail = lax.slice_in_dim(cells, cells.shape[dim] - width, cells.shape[dim], axis=dim)
        cells = jnp.concatenate(
            [
                lax.ppermute(tail, axis, [(i, (i + 1) % count) for i in range(ends)]),
                cells,
                lax.ppermute(head, axis, [((i + 1) % count, i) for i in range(ends)]),
            ],
            axis=dim,
        )
    return cells


def gelu_tanh(values):
    return jax.nn.gelu(values, approximate=True)


def attention(tokens, tok_f, norm_gain, q_weight, kv_weight, out_weight):
    token_rows = tokens.shape[0]
    normed = (
        tok_f * lax.rsqrt(jnp.mean(tok_f * tok_f, axis=-1, keepdims=True) + 1e-06) * norm_gain
    ).astype(jnp.bfloat16)
    query = jnp.dot(normed, q_weight, preferred_element_type=jnp.float32).astype(jnp.bfloat16)
    keyval = jnp.dot(normed, kv_weight, preferred_element_type=jnp.float32).astype(jnp.bfloat16)
    query_rows = query.reshape(token_rows * HEADS, QK)

    def block_update(carry, key_block):
        running_max, running_sum, weighted = carry
        scores = lax.dot_general(
            query_rows,
            key_block[:, :QK],
            (((1,), (1,)), ((), ())),
            preferred_element_type=jnp.float32,
        ) * QK ** (-0.5)
        new_max = jnp.maximum(running_max, jnp.max(scores, axis=1))
        shrink = jnp.exp(running_max - new_max)
        expw = jnp.exp(scores - new_max[:, None])
        running_sum = running_sum * shrink + jnp.sum(expw, axis=1)
        weighted = weighted * shrink[:, None] + jnp.dot(
            expw.astype(jnp.bfloat16), key_block[:, QK:], preferred_element_type=jnp.float32
        )
        return (new_max, running_sum, weighted)

    start_state = (
        jnp.full((token_rows * HEADS,), -1e30, jnp.float32),
        jnp.zeros((token_rows * HEADS,), jnp.float32),
        jnp.zeros((token_rows * HEADS, VDIM), jnp.float32),
    )
    carry = start_state
    piece = lax.all_gather(keyval, "seq", axis=0, tiled=True)
    count = piece.shape[0]

    def step_fn(inner, key_block):
        return (block_update(inner, key_block), 0)

    carry, unused = lax.scan(step_fn, carry, piece.reshape(count // 128, 128, piece.shape[1]))
    running_max, running_sum, weighted = carry
    context = (
        (weighted / running_sum[:, None]).reshape(token_rows, HEADS * VDIM).astype(jnp.bfloat16)
    )
    return (tok_f + jnp.dot(context, out_weight, preferred_element_type=jnp.float32)).astype(
        jnp.bfloat16
    )


def decoder_back(tok_f, dec_weight, track_weight, track_grad, track_index, track_mask):
    token_rows = tok_f.shape[0]
    exchanged = lax.all_to_all(track_grad, "seq", split_axis=0, concat_axis=1, tiled=True)
    masked = exchanged * track_mask.astype(jnp.bfloat16)[None, :]
    every_row = lax.all_gather(track_weight, "seq", axis=0, tiled=True)
    selected = jnp.take(every_row, track_index, axis=0)
    head_f = jnp.dot(masked, selected, preferred_element_type=jnp.float32)
    head_gradient = head_f.astype(jnp.bfloat16)
    padded_input = with_halo(head_gradient, (("seq", 0),), DILATION_SPAN).astype(jnp.float32)
    skip_act, pullback = jax.vjp(gelu_tanh, tok_f)
    convback = jnp.zeros(tok_f.shape, jnp.float32)
    tap_terms = []
    for shift_amount in range(3):
        shifted_rows = padded_input[
            DILATION_SPAN * (2 - shift_amount) : DILATION_SPAN * (2 - shift_amount) + token_rows
        ]
        convback = convback + dec_weight[shift_amount][None, :] * shifted_rows
        tap_terms.append(jnp.sum(skip_act * shifted_rows, axis=0))
    skip_grad = pullback(convback)[0].astype(jnp.bfloat16)
    summed = lax.psum(jnp.stack(tap_terms, axis=0), "seq")
    dec_weight_grad = summed / jnp.float32(math.sqrt(token_rows * lax.axis_size("seq")))
    return (skip_grad, dec_weight_grad)


def shards(
    enc_input,
    enc_weight,
    norm_gain,
    q_weight,
    kv_weight,
    out_weight,
    dec_weight,
    track_weight,
    track_grad,
    track_index,
    track_mask,
):
    token_rows = enc_input.shape[0] // 2
    patches = enc_input.reshape(token_rows, 2 * enc_input.shape[1])
    tok_sum = jnp.dot(
        patches,
        lax.all_gather(enc_weight, "seq", axis=0, tiled=True),
        preferred_element_type=jnp.float32,
    )
    tokens = tok_sum.astype(jnp.bfloat16)
    tok_f = tokens.astype(jnp.float32)
    trunk_out = attention(tokens, tok_f, norm_gain, q_weight, kv_weight, out_weight)
    skip_grad, dec_weight_grad = decoder_back(
        tok_f, dec_weight, track_weight, track_grad, track_index, track_mask
    )
    return (trunk_out, skip_grad, dec_weight_grad)


def solution(mesh):
    return jax.shard_map(
        shards,
        mesh=mesh,
        in_specs=(
            P(("groups", "seq"), None),
            P("seq", None),
            P(),
            P(),
            P(),
            P(),
            P(),
            P("seq", None),
            P("groups", "seq"),
            P("groups"),
            P("groups"),
        ),
        out_specs=(P(("groups", "seq"), None), P(("groups", "seq"), None), P("groups", None)),
        check_vma=False,
    )
```

profile of v0, /device:TPU:0, one launch (start us, length us, event | category | flops | bytes accessed | tf_op | source)
XLA Modules:
  0.0 272.7 jit_solution(8789962556055584525)
XLA Ops:
  9.6 7.4 %all-to-all-start = ((bf16[16,128,12]{1,2,0:T(8,128)(2,1)}), bf16[16,128,12]{1,2,0:T(8,128)(2,1)S(1)}, u32[]{:S(2)}, u32[]{:S(2)}) async-start(bf16[16,128,12]{1,2,0:T(8,128)(2,1)} %copy.20), calls=%async_computation | async-start | bytes 131072 | tf_op jit(solution)/shard_map/all_to_all | solution.py:84
  17.1 30.1 %all-gather = bf16[16,12,1536]{2,1,0:T(8,128)(2,1)} all-gather(bf16[1,12,1536]{2,1,0:T(8,128)(2,1)} %bitcast.28), channel_id=1, replica_groups=mesh['groups'=2,'seq'=16] {'seq'}, dimensions={0}, use_global_device_ids=true | all-gather | bytes 626688 | tf_op jit(solution)/shard_map/all_gather | solution.py:86
  47.2 2.0 reshape.51
  51.3 3.6 %gather_fusion = bf16[192,1536]{1,0:T(8,128)(2,1)} fusion(bf16[192,1536]{1,0:T(8,128)(2,1)} %reshape.51, s32[1024]{0:T(1024)S(1)} %pad_clamp_fusion), kind=kCustom, calls=%fused_computation | custom fusion | bytes 1180416 | tf_op jit(solution)/shard_map/jit(_take)/gather | solution.py:87
  55.5 1.5 convolution_convert_fusion.1
  57.7 2.8 %collective-permute-start = (bf16[8,1536]{1,0:T(8,128)(2,1)}, bf16[8,1536]{1,0:T(8,128)(2,1)}, u32[]{:S(2)}, u32[]{:S(2)}) collective-permute-start(bf16[8,1536]{1,0:T(8,128)(2,1)} %get-tuple-element.101), channel_id=1, source_target_pairs={{0,1},{1,2},{2,3},{3,4},{4,5},{5,6},{6,7},{7,8},{8,9},{9,10},{10,1... | collective-permute-start | bytes 73736 | tf_op jit(solution)/shard_map/ppermute | solution.py:21
  60.5 1.3 collective-permute-start.1
  61.7 1.5 slice_reduce_fusion.2
  63.2 2.1 reshape.38
  65.4 1.8 maximum_convert_fusion
  67.2 26.1 %all-gather.4.cloned.1.call-done = bf16[2816,1536]{1,0:T(8,128)(2,1)} async-done(((bf16[176,1536]{1,0:T(8,128)(2,1)}), bf16[2816,1536]{1,0:T(8,128)(2,1)}) %all-gather.4.cloned.1.call-update) | async-done | bytes 8650768 | tf_op jit(solution)/shard_map/all_gather | solution.py:123
  93.3 7.5 %multiply_reduce_fusion.3 = (f32[1536]{0:T(1024)S(1)}, f32[1536]{0:T(1024)S(1)}, f32[1536]{0:T(1024)S(1)}, f32[128]{0:T(128)S(1)}, bf16[128,1536]{1,0:T(8,128)(2,1)}, /*index=5*/f32[128,1536]{1,0:T(8,128)S(1)}) fusion(f32[144,1536]{1,0:T(8,128)} %maximum_convert_fusion, f32[1536]{0:T(1024)S(1)} %get-tuple-element.82, f32[1536]{0:T(1024)} %get-tuple-element.83, ...), kind=kOutput, calls=%fused_computation.34 | convolution fusion | flops 1114172800 | bytes 12947968 | tf_op jit(solution)/shard_map/dot_general | solution.py:121
  102.8 2.5 convolution_convert_fusion.2
  106.4 59.2 %psum.7 = f32[3,1536]{1,0:T(4,128)S(1)} all-reduce(f32[3,1536]{1,0:T(4,128)S(1)} %pad_maximum_fusion), channel_id=1, replica_groups=mesh['groups'=2,'seq'=16] {'seq'}, use_global_device_ids=true, to_apply=%region_8.9 | all-reduce | flops 4608 | bytes 36864 | tf_op jit(solution)/shard_map/psum | solution.py:101
  166.2 2.6 copy.21
  168.7 89.4 %while.15 = (s32[]{:T(128)}, f32[1024]{0:T(1024)S(1)}, f32[1024]{0:T(1024)S(1)}, f32[1024,192]{0,1:T(8,128)}, bf16[16,128,320]{2,1,0:T(8,128)(2,1)}, /*index=5*/bf16[1024,128]{1,0:T(8,128)(2,1)S(1)}, s32[]{:T(128)}, s32[]{:T(128)}) while((s32[]{:T(128)}, f32[1024]{0:T(1024)S(1)}, f32[1024]{0:T(1024)S(1)}, f32[1024,192]{0,1:T(8,128)}, ...), condition=%wide.region_4.5_spmd.clone, body=%wide.region_1.4_spmd.clone.sunk | while | flops 85267456 | bytes 3735653 | solution.py:72
  170.7 1.1 fusion.41
  171.9 2.2 convolution_add_fusion.3
  176.1 1.1 fusion.41
  177.2 2.5 convolution_add_fusion.3
  181.7 1.1 fusion.41
  182.8 2.5 convolution_add_fusion.3
  187.3 1.1 fusion.41
  188.4 2.5 convolution_add_fusion.3
  192.9 1.1 fusion.41
  194.0 2.5 convolution_add_fusion.3
  198.5 1.1 fusion.41
  199.6 2.5 convolution_add_fusion.3
  204.1 1.1 fusion.41
  205.2 2.5 convolution_add_fusion.3
  209.7 1.1 fusion.41
  210.8 2.5 convolution_add_fusion.3
  215.3 1.1 fusion.41
  216.4 2.5 convolution_add_fusion.3
  220.9 1.1 fusion.41
  222.0 2.5 convolution_add_fusion.3
  226.5 1.1 fusion.41
  227.6 2.5 convolution_add_fusion.3
  232.1 1.1 fusion.41
  233.2 2.5 convolution_add_fusion.3
  237.7 1.1 fusion.41
  238.8 2.5 convolution_add_fusion.3
  244.4 2.5 convolution_add_fusion.3
  250.0 2.5 convolution_add_fusion.3
  255.6 2.5 convolution_add_fusion.3
  258.1 1.2 divide_convert_fusion
  260.3 1.5 convert_element_type.46
  261.8 4.1 %fusion.8 = bf16[128,1536]{1,0:T(8,128)(2,1)} fusion(f32[128,1536]{1,0:T(8,128)} %copy-done.1, bf16[128,1536]{1,0:T(8,128)(2,1)S(1)} %convert_element_type.46, bf16[1536,1536]{1,0:T(8,128)(2,1)} %param.18), kind=kOutput, calls=%fused_computation.19 | convolution fusion | flops 604372992 | bytes 6291456 | tf_op jit(solution)/shard_map/dot_general | solution.py:77
  (120 shorter events, 45.3 us)
Async XLA Ops:
  7.2 95.6 %copy-start = (bf16[1536,1024]{1,0:T(8,128)(2,1)S(1)}, bf16[1536,1024]{1,0:T(8,128)(2,1)}, u32[]{:S(2)}) copy-start(bf16[1536,1024]{1,0:T(8,128)(2,1)} %param.16) | copy-start | bytes 9437188
  7.2 86.1 %all-gather.4.cloned.1.call-start = ((), (), s32[]{:S(2)}) async-start(), calls=%async_computation.1 | async-start | bytes 9191424 | tf_op jit(solution)/shard_map/all_gather | solution.py:123
  9.6 45.3 %all-to-all-start = ((bf16[16,128,12]{1,2,0:T(8,128)(2,1)}), bf16[16,128,12]{1,2,0:T(8,128)(2,1)S(1)}, u32[]{:S(2)}, u32[]{:S(2)}) async-start(bf16[16,128,12]{1,2,0:T(8,128)(2,1)} %copy.20), calls=%async_computation | async-start | bytes 131072 | tf_op jit(solution)/shard_map/all_to_all | solution.py:84
  17.0 149.2 %all-gather.6.cloned.1.call-start = ((), (), s32[]{:S(2)}) async-start(), calls=%async_computation.2 | async-start | bytes 1392640 | tf_op jit(solution)/shard_map/all_gather | solution.py:66
  57.7 7.7 %collective-permute-start = (bf16[8,1536]{1,0:T(8,128)(2,1)}, bf16[8,1536]{1,0:T(8,128)(2,1)}, u32[]{:S(2)}, u32[]{:S(2)}) collective-permute-start(bf16[8,1536]{1,0:T(8,128)(2,1)} %get-tuple-element.101), channel_id=1, source_target_pairs={{0,1},{1,2},{2,3},{3,4},{4,5},{5,6},{6,7},{7,8},{8,9},{9,10},{10,1... | collective-permute-start | bytes 73736 | tf_op jit(solution)/shard_map/ppermute | solution.py:21
  60.5 4.9 %collective-permute-start.1 = (bf16[8,1536]{1,0:T(8,128)(2,1)}, bf16[8,1536]{1,0:T(8,128)(2,1)}, u32[]{:S(2)}, u32[]{:S(2)}) collective-permute-start(bf16[8,1536]{1,0:T(8,128)(2,1)} %get-tuple-element.102), channel_id=1, source_target_pairs={{1,0},{2,1},{3,2},{4,3},{5,4},{6,5},{7,6},{8,7},{9,8},{10,9},{11,1... | collective-permute-start | bytes 73736 | tf_op jit(solution)/shard_map/ppermute | solution.py:23
  93.3 8.3 %copy-start.2 = (bf16[1536,320]{0,1:T(8,128)(2,1)S(1)}, bf16[1536,320]{0,1:T(8,128)(2,1)}, u32[]{:S(2)}) copy-start(bf16[1536,320]{0,1:T(8,128)(2,1)} %param.17) | copy-start | bytes 2949124
  93.3 8.3 %copy-start.3 = (f32[1536]{0:T(1024)S(1)}, f32[1536]{0:T(1024)}, u32[]{:S(2)}) copy-start(f32[1536]{0:T(1024)} %param.15) | copy-start | bytes 18436
  100.7 0.9 copy-start.1
Sparse Core Ops, SparseCore 0:
  10.3 82.9 all-gather.3
  102.9 36.2 all-gather.5
where the time goes:
time: 275 us; the launch traced here: 273 us
  blocking collectives  89.3 us (32%)
  matrix products  72.9 us (27%)
  local copies, waits for them, and re-layouts  33.7 us (12%)
  waiting for transfers between devices  26.8 us (10%)
  other arithmetic  24.2 us (9%)
  between operations  14.2 us (5%)
  starting transfers between devices  11.6 us (4%)
    psum x1, blocking collectives, decoder_back(): summed = lax.psum(jnp.stack(tap_terms, axis=0), 'seq')  59.2 us
    dot_general x16, matrix products, block_update(): jnp.dot(expw.astype(jnp.bfloat16), key_block[:, QK:], preferred_element_t...  39.6 us
    all_gather x1, blocking collectives, decoder_back(): every_row = lax.all_gather(track_weight, 'seq', axis=0, tiled=True)  30.1 us
    all_gather x1, waiting for transfers between devices, shards(): lax.all_gather(enc_weight, 'seq', axis=0, tiled=True)  26.1 us
    reduce_sum x16, other arithmetic, block_update(): running_sum = running_sum * shrink + jnp.sum(expw, axis=1)  18.2 us
    dot_general x16, matrix products, block_update(): lax.dot_general(query_rows, key_block[:, :QK], (((1,), (1,)), ((), ())),...  16.7 us
    squeeze x16, local copies, waits for them, and re-layouts, attention(): lax.scan(step_fn, carry, piece.reshape(count // 128, 128, piece.shape[1]))  14.4 us
    dot_general x1, matrix products, shards(): jnp.dot(patches, lax.all_gather(enc_weight, 'seq', axis=0, tiled=True), p...  7.46 us
  transfers between devices with their start and end apart: 5, of which 1 were waited for; matrix products, arithmetic and copies ran while one was open for 8% of the time, Pallas kernels for 0%

commit v1 on v0

--- a/solution.py
+++ b/solution.py
@@ -8,6 +8,22 @@
 QK = 128
 VDIM = 192
 DILATION_SPAN = 8
+
+
+def collect(x, axis, dim):
+    ways, here, step = (lax.axis_size(axis), lax.axis_index(axis), x.shape[dim])
+    dims = [n * ways if d == dim else n for d, n in enumerate(x.shape)]
+    full = lax.dynamic_update_slice_in_dim(jnp.zeros(dims, x.dtype), x, here * step, axis=dim)
+    going_up = going_down = x
+    for far in range(1, ways // 2 + 1):
+        going_up = lax.ppermute(going_up, axis, [(d, (d + 1) % ways) for d in range(ways)])
+        full = lax.dynamic_update_slice_in_dim(full, going_up, (here - far) % ways * step, axis=dim)
+        if 2 * far < ways:
+            going_down = lax.ppermute(going_down, axis, [(d, (d - 1) % ways) for d in range(ways)])
+            full = lax.dynamic_update_slice_in_dim(
+                full, going_down, (here + far) % ways * step, axis=dim
+            )
+    return full
 
 
 def with_halo(cells, sides, width):
@@ -83,7 +99,7 @@
     token_rows = tok_f.shape[0]
     exchanged = lax.all_to_all(track_grad, "seq", split_axis=0, concat_axis=1, tiled=True)
     masked = exchanged * track_mask.astype(jnp.bfloat16)[None, :]
-    every_row = lax.all_gather(track_weight, "seq", axis=0, tiled=True)
+    every_row = collect(track_weight, "seq", 0)
     selected = jnp.take(every_row, track_index, axis=0)
     head_f = jnp.dot(masked, selected, preferred_element_type=jnp.float32)
     head_gradient = head_f.astype(jnp.bfloat16)

time: 275 us -> 291 us (1.058)
  starting transfers between devices: 11.6 us -> 41.5 us
  blocking collectives: 89.3 us -> 64.1 us
  local copies, waits for them, and re-layouts: 33.7 us -> 57.3 us
  waiting for transfers between devices: 26.8 us -> 11.8 us
    ppermute x0 -> x15, starting transfers between devices: none -> 32.5 us  [the longest x7 32 us: collect(): lax.ppermute(going_down, axis, [(d, (d - 1) % ways) for d in range(ways)])]
    all_gather x1 -> x0, blocking collectives: 30.1 us -> none  [decoder_back(): every_row = lax.all_gather(track_weight, 'seq', axis=0, tiled=True)]
    all_gather x1, waiting for transfers between devices: 26.1 us -> 0.01 us  [shards(): lax.all_gather(enc_weight, 'seq', axis=0, tiled=True)]
    dynamic_update_slice x0 -> x16, local copies, waits for them, and re-layouts: none -> 24.1 us  [the longest x8 12 us: collect(): lax.dynamic_update_slice_in_dim(full, going_up, (here - far) % ways * ste...]
    ppermute x0 -> x15, waiting for transfers between devices: none -> 11 us  [the longest x8 8.22 us: collect(): lax.ppermute(going_up, axis, [(d, (d + 1) % ways) for d in range(ways)])]
    psum x1, blocking collectives: 59.2 us -> 64.1 us  [decoder_back(): summed = lax.psum(jnp.stack(tap_terms, axis=0), 'seq')]
    unnamed x11 -> x18, local copies, waits for them, and re-layouts: 6.52 us -> 4.94 us
  transfers between devices with their start and end apart: 5 -> 20, of which waited for: 1 -> 7; matrix products, arithmetic and copies ran while one was open for 8% -> 16% of each run, Pallas kernels for 0% -> 0%
where the time goes in v1:
time: 291 us; the launch traced here: 287 us
  matrix products  72.4 us (25%)
  blocking collectives  64.1 us (22%)
  local copies, waits for them, and re-layouts  57.3 us (20%)
  starting transfers between devices  41.5 us (14%)
  other arithmetic  25.9 us (9%)
  between operations  14.2 us (5%)
  waiting for transfers between devices  11.8 us (4%)
    psum x1, blocking collectives, decoder_back(): summed = lax.psum(jnp.stack(tap_terms, axis=0), 'seq')  64.1 us
    dot_general x16, matrix products, block_update(): jnp.dot(expw.astype(jnp.bfloat16), key_block[:, QK:], preferred_element_t...  39.4 us
    ppermute x7, starting transfers between devices, collect(): lax.ppermute(going_down, axis, [(d, (d - 1) % ways) for d in range(ways)])  32 us
    reduce_sum x16, other arithmetic, block_update(): running_sum = running_sum * shrink + jnp.sum(expw, axis=1)  18.2 us
    dot_general x16, matrix products, block_update(): lax.dot_general(query_rows, key_block[:, :QK], (((1,), (1,)), ((), ())),...  16.3 us
    squeeze x16, local copies, waits for them, and re-layouts, attention(): lax.scan(step_fn, carry, piece.reshape(count // 128, 128, piece.shape[1]))  14.4 us
    dynamic_update_slice x8, local copies, waits for them, and re-layouts, collect(): lax.dynamic_update_slice_in_dim(full, going_up, (here - far) % ways * ste...  12 us
    dynamic_update_slice x7, local copies, waits for them, and re-layouts, collect(): lax.dynamic_update_slice_in_dim(full, going_down, (here + far) % ways * s...  10.6 us
  transfers between devices with their start and end apart: 20, of which 7 were waited for; matrix products, arithmetic and copies ran while one was open for 16% of the time, Pallas kernels for 0%

profile of v1, /device:TPU:0, one launch (start us, length us, event | category | flops | bytes accessed | tf_op | source)
XLA Modules:
  0.0 287.3 jit_solution(6974486364475899879)
XLA Ops:
  8.4 5.1 %collective-permute-start.1 = (bf16[12,1536]{1,0:T(8,128)(2,1)}, bf16[12,1536]{1,0:T(8,128)(2,1)S(1)}, u32[]{:S(2)}, u32[]{:S(2)}) collective-permute-start(bf16[12,1536]{1,0:T(8,128)(2,1)} %param.20), channel_id=1, source_target_pairs={{0,15},{1,0},{2,1},{3,2},{4,3},{5,4},{6,5},{7,6},{8,7},{9,8},{10,9... | collective-permute-start | bytes 110600 | tf_op jit(solution)/shard_map/ppermute | solution.py:22
  13.5 2.0 collective-permute-done
  15.5 4.4 %collective-permute-start.3 = (bf16[12,1536]{1,0:T(8,128)(2,1)S(1)}, bf16[12,1536]{1,0:T(8,128)(2,1)S(1)}, u32[]{:S(2)}, u32[]{:S(2)}) collective-permute-start(bf16[12,1536]{1,0:T(8,128)(2,1)S(1)} %collective-permute-done.1), channel_id=1, source_target_pairs={{0,15},{1,0},{2,1},{3,2},{4,3},{5,4},{6,5},{7,6},{8,7},{9,8},{10,9... | collective-permute-start | bytes 110600 | tf_op jit(solution)/shard_map/ppermute | solution.py:22
  19.9 1.8 collective-permute-done.2
  21.7 4.4 %collective-permute-start.5 = (bf16[12,1536]{1,0:T(8,128)(2,1)S(1)}, bf16[12,1536]{1,0:T(8,128)(2,1)S(1)}, u32[]{:S(2)}, u32[]{:S(2)}) collective-permute-start(bf16[12,1536]{1,0:T(8,128)(2,1)S(1)} %collective-permute-done.3), channel_id=1, source_target_pairs={{0,15},{1,0},{2,1},{3,2},{4,3},{5,4},{6,5},{7,6},{8,7},{9,8},{10,9... | collective-permute-start | bytes 110600 | tf_op jit(solution)/shard_map/ppermute | solution.py:22
  26.1 2.6 collective-permute-done.4
  29.6 4.5 %collective-permute-start.7 = (bf16[12,1536]{1,0:T(8,128)(2,1)S(1)}, bf16[12,1536]{1,0:T(8,128)(2,1)}, u32[]{:S(2)}, u32[]{:S(2)}) collective-permute-start(bf16[12,1536]{1,0:T(8,128)(2,1)S(1)} %collective-permute-done.5), channel_id=1, source_target_pairs={{0,15},{1,0},{2,1},{3,2},{4,3},{5,4},{6,5},{7,6},{8,7},{9,8},{10,9... | collective-permute-start | bytes 110600 | tf_op jit(solution)/shard_map/ppermute | solution.py:22
  34.1 1.9 collective-permute-done.6
  36.6 5.8 %all-to-all-start = ((bf16[16,128,12]{1,2,0:T(8,128)(2,1)}), bf16[16,128,12]{1,2,0:T(8,128)(2,1)S(1)}, u32[]{:S(2)}, u32[]{:S(2)}) async-start(bf16[16,128,12]{1,2,0:T(8,128)(2,1)} %copy.17), calls=%async_computation | async-start | bytes 131072 | tf_op jit(solution)/shard_map/all_to_all | solution.py:100
  42.5 4.4 %collective-permute-start.9 = (bf16[12,1536]{1,0:T(8,128)(2,1)}, bf16[12,1536]{1,0:T(8,128)(2,1)S(1)}, u32[]{:S(2)}, u32[]{:S(2)}) collective-permute-start(bf16[12,1536]{1,0:T(8,128)(2,1)} %collective-permute-done.7), channel_id=1, source_target_pairs={{0,15},{1,0},{2,1},{3,2},{4,3},{5,4},{6,5},{7,6},{8,7},{9,8},{10,9... | collective-permute-start | bytes 110600 | tf_op jit(solution)/shard_map/ppermute | solution.py:22
  49.6 4.4 %collective-permute-start.11 = (bf16[12,1536]{1,0:T(8,128)(2,1)S(1)}, bf16[12,1536]{1,0:T(8,128)(2,1)}, u32[]{:S(2)}, u32[]{:S(2)}) collective-permute-start(bf16[12,1536]{1,0:T(8,128)(2,1)S(1)} %collective-permute-done.9), channel_id=1, source_target_pairs={{0,15},{1,0},{2,1},{3,2},{4,3},{5,4},{6,5},{7,6},{8,7},{9,8},{10,9... | collective-permute-start | bytes 110600 | tf_op jit(solution)/shard_map/ppermute | solution.py:22
  56.7 4.7 %collective-permute-start.13 = (bf16[12,1536]{1,0:T(8,128)(2,1)}, bf16[12,1536]{1,0:T(8,128)(2,1)}, u32[]{:S(2)}, u32[]{:S(2)}) collective-permute-start(bf16[12,1536]{1,0:T(8,128)(2,1)} %collective-permute-done.11), channel_id=1, source_target_pairs={{0,15},{1,0},{2,1},{3,2},{4,3},{5,4},{6,5},{7,6},{8,7},{9,8},{10,9... | collective-permute-start | bytes 110600 | tf_op jit(solution)/shard_map/ppermute | solution.py:22
  64.1 1.5 dynamic_update_slice.48
  76.7 1.5 dynamic_update_slice.56
  78.2 1.5 dynamic_update_slice.57
  79.7 1.5 dynamic_update_slice.58
  81.2 1.5 dynamic_update_slice.59
  82.8 1.5 dynamic_update_slice.60
  84.3 1.5 dynamic_update_slice.61
  85.8 1.5 dynamic_update_slice.62
  87.4 1.5 dynamic_update_slice.63
  88.9 3.8 %gather_fusion = bf16[192,1536]{1,0:T(8,128)(2,1)} fusion(bf16[192,1536]{1,0:T(8,128)(2,1)} %dynamic_update_slice.63, s32[1024]{0:T(1024)} %pad_clamp_fusion), kind=kCustom, calls=%fused_computation | custom fusion | bytes 1180416 | tf_op jit(solution)/shard_map/jit(_take)/gather | solution.py:103
  94.8 1.9 collective-permute-start.15
  99.4 2.1 reshape.38
  101.5 1.9 maximum_convert_fusion
  103.4 7.5 %multiply_reduce_fusion.3 = (f32[1536]{0:T(1024)S(1)}, f32[1536]{0:T(1024)S(1)}, f32[1536]{0:T(1024)S(1)}, f32[128]{0:T(128)S(1)}, bf16[128,1536]{1,0:T(8,128)(2,1)}, /*index=5*/f32[128,1536]{1,0:T(8,128)S(1)}) fusion(f32[144,1536]{1,0:T(8,128)} %maximum_convert_fusion, f32[1536]{0:T(1024)S(1)} %get-tuple-element.76, f32[1536]{0:T(1024)} %get-tuple-element.77, ...), kind=kOutput, calls=%fused_computation.34 | convolution fusion | flops 1114172800 | bytes 12947968 | tf_op jit(solution)/shard_map/dot_general | solution.py:137
  113.0 2.5 convolution_convert_fusion.2
  116.6 64.1 %psum.7 = f32[3,1536]{1,0:T(4,128)S(1)} all-reduce(f32[3,1536]{1,0:T(4,128)S(1)} %pad_maximum_fusion), channel_id=1, replica_groups=mesh['groups'=2,'seq'=16] {'seq'}, use_global_device_ids=true, to_apply=%region_8.9 | all-reduce | flops 4608 | bytes 36864 | tf_op jit(solution)/shard_map/psum | solution.py:117
  181.3 2.6 copy.18
  183.8 88.8 %while.15 = (s32[]{:T(128)}, f32[1024]{0:T(1024)S(1)}, f32[1024]{0:T(1024)S(1)}, f32[1024,192]{0,1:T(8,128)}, bf16[16,128,320]{2,1,0:T(8,128)(2,1)}, /*index=5*/bf16[1024,128]{1,0:T(8,128)(2,1)S(1)}, s32[]{:T(128)}, s32[]{:T(128)}) while((s32[]{:T(128)}, f32[1024]{0:T(1024)S(1)}, f32[1024]{0:T(1024)S(1)}, f32[1024,192]{0,1:T(8,128)}, ...), condition=%wide.region_4.5_spmd.clone, body=%wide.region_1.4_spmd.clone.sunk | while | flops 85267456 | bytes 3735653 | solution.py:88
  186.9 2.2 convolution_add_fusion.3
  192.2 2.5 convolution_add_fusion.3
  197.8 2.5 convolution_add_fusion.3
  203.4 2.5 convolution_add_fusion.3
  208.9 2.5 convolution_add_fusion.3
  214.5 2.5 convolution_add_fusion.3
  220.1 2.5 convolution_add_fusion.3
  225.6 2.5 convolution_add_fusion.3
  231.2 2.5 convolution_add_fusion.3
  236.8 2.5 convolution_add_fusion.3
  242.3 2.5 convolution_add_fusion.3
  247.9 2.5 convolution_add_fusion.3
  253.5 2.5 convolution_add_fusion.3
  259.0 2.5 convolution_add_fusion.3
  264.6 2.5 convolution_add_fusion.3
  270.2 2.5 convolution_add_fusion.3
  274.9 1.5 convert_element_type.46
  276.4 4.1 %fusion.8 = bf16[128,1536]{1,0:T(8,128)(2,1)} fusion(f32[128,1536]{1,0:T(8,128)} %copy-done.1, bf16[128,1536]{1,0:T(8,128)(2,1)S(1)} %convert_element_type.46, bf16[1536,1536]{1,0:T(8,128)(2,1)} %param.18), kind=kOutput, calls=%fused_computation.19 | convolution fusion | flops 604372992 | bytes 6291456 | tf_op jit(solution)/shard_map/dot_general | solution.py:93
  (173 shorter events, 81.9 us)
Async XLA Ops:
  7.2 105.9 %copy-start = (bf16[1536,1024]{1,0:T(8,128)(2,1)S(1)}, bf16[1536,1024]{1,0:T(8,128)(2,1)}, u32[]{:S(2)}) copy-start(bf16[1536,1024]{1,0:T(8,128)(2,1)} %param.16) | copy-start | bytes 9437188
  7.2 96.2 %all-gather.3.cloned.1.call-start = ((), (), s32[]{:S(2)}) async-start(), calls=%async_computation.1 | async-start | bytes 9191424 | tf_op jit(solution)/shard_map/all_gather | solution.py:139
  7.9 7.6 %collective-permute-start = (bf16[12,1536]{1,0:T(8,128)(2,1)}, bf16[12,1536]{1,0:T(8,128)(2,1)S(1)}, u32[]{:S(2)}, u32[]{:S(2)}) collective-permute-start(bf16[12,1536]{1,0:T(8,128)(2,1)} %param.20), channel_id=1, source_target_pairs={{0,1},{1,2},{2,3},{3,4},{4,5},{5,6},{6,7},{7,8},{8,9},{9,10},{10,1... | collective-permute-start | bytes 110600 | tf_op jit(solution)/shard_map/ppermute | solution.py:19
  8.4 7.1 %collective-permute-start.1 = (bf16[12,1536]{1,0:T(8,128)(2,1)}, bf16[12,1536]{1,0:T(8,128)(2,1)S(1)}, u32[]{:S(2)}, u32[]{:S(2)}) collective-permute-start(bf16[12,1536]{1,0:T(8,128)(2,1)} %param.20), channel_id=1, source_target_pairs={{0,15},{1,0},{2,1},{3,2},{4,3},{5,4},{6,5},{7,6},{8,7},{9,8},{10,9... | collective-permute-start | bytes 110600 | tf_op jit(solution)/shard_map/ppermute | solution.py:22
  15.5 6.2 %collective-permute-start.2 = (bf16[12,1536]{1,0:T(8,128)(2,1)S(1)}, bf16[12,1536]{1,0:T(8,128)(2,1)S(1)}, u32[]{:S(2)}, u32[]{:S(2)}) collective-permute-start(bf16[12,1536]{1,0:T(8,128)(2,1)S(1)} %collective-permute-done), channel_id=1, source_target_pairs={{0,1},{1,2},{2,3},{3,4},{4,5},{5,6},{6,7},{7,8},{8,9},{9,10},{10,1... | collective-permute-start | bytes 110600 | tf_op jit(solution)/shard_map/ppermute | solution.py:19
  15.5 6.2 %collective-permute-start.3 = (bf16[12,1536]{1,0:T(8,128)(2,1)S(1)}, bf16[12,1536]{1,0:T(8,128)(2,1)S(1)}, u32[]{:S(2)}, u32[]{:S(2)}) collective-permute-start(bf16[12,1536]{1,0:T(8,128)(2,1)S(1)} %collective-permute-done.1), channel_id=1, source_target_pairs={{0,15},{1,0},{2,1},{3,2},{4,3},{5,4},{6,5},{7,6},{8,7},{9,8},{10,9... | collective-permute-start | bytes 110600 | tf_op jit(solution)/shard_map/ppermute | solution.py:22
  21.7 7.0 %collective-permute-start.4 = (bf16[12,1536]{1,0:T(8,128)(2,1)S(1)}, bf16[12,1536]{1,0:T(8,128)(2,1)S(1)}, u32[]{:S(2)}, u32[]{:S(2)}) collective-permute-start(bf16[12,1536]{1,0:T(8,128)(2,1)S(1)} %collective-permute-done.2), channel_id=1, source_target_pairs={{0,1},{1,2},{2,3},{3,4},{4,5},{5,6},{6,7},{7,8},{8,9},{9,10},{10,1... | collective-permute-start | bytes 110600 | tf_op jit(solution)/shard_map/ppermute | solution.py:19
  21.7 7.9 %collective-permute-start.5 = (bf16[12,1536]{1,0:T(8,128)(2,1)S(1)}, bf16[12,1536]{1,0:T(8,128)(2,1)S(1)}, u32[]{:S(2)}, u32[]{:S(2)}) collective-permute-start(bf16[12,1536]{1,0:T(8,128)(2,1)S(1)} %collective-permute-done.3), channel_id=1, source_target_pairs={{0,15},{1,0},{2,1},{3,2},{4,3},{5,4},{6,5},{7,6},{8,7},{9,8},{10,9... | collective-permute-start | bytes 110600 | tf_op jit(solution)/shard_map/ppermute | solution.py:22
  28.7 7.2 %collective-permute-start.6 = (bf16[12,1536]{1,0:T(8,128)(2,1)S(1)}, bf16[12,1536]{1,0:T(8,128)(2,1)S(1)}, u32[]{:S(2)}, u32[]{:S(2)}) collective-permute-start(bf16[12,1536]{1,0:T(8,128)(2,1)S(1)} %collective-permute-done.4), channel_id=1, source_target_pairs={{0,1},{1,2},{2,3},{3,4},{4,5},{5,6},{6,7},{7,8},{8,9},{9,10},{10,1... | collective-permute-start | bytes 110600 | tf_op jit(solution)/shard_map/ppermute | solution.py:19
  29.6 12.9 %collective-permute-start.7 = (bf16[12,1536]{1,0:T(8,128)(2,1)S(1)}, bf16[12,1536]{1,0:T(8,128)(2,1)}, u32[]{:S(2)}, u32[]{:S(2)}) collective-permute-start(bf16[12,1536]{1,0:T(8,128)(2,1)S(1)} %collective-permute-done.5), channel_id=1, source_target_pairs={{0,15},{1,0},{2,1},{3,2},{4,3},{5,4},{6,5},{7,6},{8,7},{9,8},{10,9... | collective-permute-start | bytes 110600 | tf_op jit(solution)/shard_map/ppermute | solution.py:22
  35.9 11.0 %collective-permute-start.8 = (bf16[12,1536]{1,0:T(8,128)(2,1)S(1)}, bf16[12,1536]{1,0:T(8,128)(2,1)}, u32[]{:S(2)}, u32[]{:S(2)}) collective-permute-start(bf16[12,1536]{1,0:T(8,128)(2,1)S(1)} %collective-permute-done.6), channel_id=1, source_target_pairs={{0,1},{1,2},{2,3},{3,4},{4,5},{5,6},{6,7},{7,8},{8,9},{9,10},{10,1... | collective-permute-start | bytes 110600 | tf_op jit(solution)/shard_map/ppermute | solution.py:19
  36.6 34.9 %all-to-all-start = ((bf16[16,128,12]{1,2,0:T(8,128)(2,1)}), bf16[16,128,12]{1,2,0:T(8,128)(2,1)S(1)}, u32[]{:S(2)}, u32[]{:S(2)}) async-start(bf16[16,128,12]{1,2,0:T(8,128)(2,1)} %copy.17), calls=%async_computation | async-start | bytes 131072 | tf_op jit(solution)/shard_map/all_to_all | solution.py:100
  42.4 138.8 %all-gather.5.cloned.1.call-start = ((), (), s32[]{:S(2)}) async-start(), calls=%async_computation.2 | async-start | bytes 1392640 | tf_op jit(solution)/shard_map/all_gather | solution.py:82
  42.5 6.5 %collective-permute-start.9 = (bf16[12,1536]{1,0:T(8,128)(2,1)}, bf16[12,1536]{1,0:T(8,128)(2,1)S(1)}, u32[]{:S(2)}, u32[]{:S(2)}) collective-permute-start(bf16[12,1536]{1,0:T(8,128)(2,1)} %collective-permute-done.7), channel_id=1, source_target_pairs={{0,15},{1,0},{2,1},{3,2},{4,3},{5,4},{6,5},{7,6},{8,7},{9,8},{10,9... | collective-permute-start | bytes 110600 | tf_op jit(solution)/shard_map/ppermute | solution.py:22
  46.9 7.1 %collective-permute-start.10 = (bf16[12,1536]{1,0:T(8,128)(2,1)}, bf16[12,1536]{1,0:T(8,128)(2,1)S(1)}, u32[]{:S(2)}, u32[]{:S(2)}) collective-permute-start(bf16[12,1536]{1,0:T(8,128)(2,1)} %collective-permute-done.8), channel_id=1, source_target_pairs={{0,1},{1,2},{2,3},{3,4},{4,5},{5,6},{6,7},{7,8},{8,9},{9,10},{10,1... | collective-permute-start | bytes 110600 | tf_op jit(solution)/shard_map/ppermute | solution.py:19
  49.0 0.6 copy-start.3
  49.6 7.1 %collective-permute-start.11 = (bf16[12,1536]{1,0:T(8,128)(2,1)S(1)}, bf16[12,1536]{1,0:T(8,128)(2,1)}, u32[]{:S(2)}, u32[]{:S(2)}) collective-permute-start(bf16[12,1536]{1,0:T(8,128)(2,1)S(1)} %collective-permute-done.9), channel_id=1, source_target_pairs={{0,15},{1,0},{2,1},{3,2},{4,3},{5,4},{6,5},{7,6},{8,7},{9,8},{10,9... | collective-permute-start | bytes 110600 | tf_op jit(solution)/shard_map/ppermute | solution.py:22
  54.1 2.7 copy-start.4
  54.1 7.4 %collective-permute-start.12 = (bf16[12,1536]{1,0:T(8,128)(2,1)S(1)}, bf16[12,1536]{1,0:T(8,128)(2,1)}, u32[]{:S(2)}, u32[]{:S(2)}) collective-permute-start(bf16[12,1536]{1,0:T(8,128)(2,1)S(1)} %collective-permute-done.10), channel_id=1, source_target_pairs={{0,1},{1,2},{2,3},{3,4},{4,5},{5,6},{6,7},{7,8},{8,9},{9,10},{10,1... | collective-permute-start | bytes 110600 | tf_op jit(solution)/shard_map/ppermute | solution.py:19
  56.7 29.1 %collective-permute-start.13 = (bf16[12,1536]{1,0:T(8,128)(2,1)}, bf16[12,1536]{1,0:T(8,128)(2,1)}, u32[]{:S(2)}, u32[]{:S(2)}) collective-permute-start(bf16[12,1536]{1,0:T(8,128)(2,1)} %collective-permute-done.11), channel_id=1, source_target_pairs={{0,15},{1,0},{2,1},{3,2},{4,3},{5,4},{6,5},{7,6},{8,7},{9,8},{10,9... | collective-permute-start | bytes 110600 | tf_op jit(solution)/shard_map/ppermute | solution.py:22
  61.5 25.9 %collective-permute-start.14 = (bf16[12,1536]{1,0:T(8,128)(2,1)}, bf16[12,1536]{1,0:T(8,128)(2,1)}, u32[]{:S(2)}, u32[]{:S(2)}) collective-permute-start(bf16[12,1536]{1,0:T(8,128)(2,1)} %collective-permute-done.12), channel_id=1, source_target_pairs={{0,1},{1,2},{2,3},{3,4},{4,5},{5,6},{6,7},{7,8},{8,9},{9,10},{10,1... | collective-permute-start | bytes 110600 | tf_op jit(solution)/shard_map/ppermute | solution.py:19
  76.7 16.0 %copy-start.6 = (pred[192]{0:T(512)(128)(4,1)S(1)}, pred[192]{0:T(512)(128)(4,1)}, u32[]{:S(2)}) copy-start(pred[192]{0:T(512)(128)(4,1)} %compare_and_fusion) | copy-start | bytes 580
  76.7 16.0 %copy-start.7 = (bf16[192]{0:T(256)(128)(2,1)S(1)}, bf16[192]{0:T(256)(128)(2,1)}, u32[]{:S(2)}) copy-start(bf16[192]{0:T(256)(128)(2,1)} %convert_element_type.48) | copy-start | bytes 1156
  94.8 6.8 %collective-permute-start.15 = (bf16[8,1536]{1,0:T(8,128)(2,1)}, bf16[8,1536]{1,0:T(8,128)(2,1)}, u32[]{:S(2)}, u32[]{:S(2)}) collective-permute-start(bf16[8,1536]{1,0:T(8,128)(2,1)} %get-tuple-element.95), channel_id=1, source_target_pairs={{0,1},{1,2},{2,3},{3,4},{4,5},{5,6},{6,7},{7,8},{8,9},{9,10},{10,1... | collective-permute-start | bytes 73736 | tf_op jit(solution)/shard_map/ppermute | solution.py:37
  96.7 4.9 %collective-permute-start.16 = (bf16[8,1536]{1,0:T(8,128)(2,1)}, bf16[8,1536]{1,0:T(8,128)(2,1)}, u32[]{:S(2)}, u32[]{:S(2)}) collective-permute-start(bf16[8,1536]{1,0:T(8,128)(2,1)} %get-tuple-element.96), channel_id=1, source_target_pairs={{1,0},{2,1},{3,2},{4,3},{5,4},{6,5},{7,6},{8,7},{9,8},{10,9},{11,1... | collective-permute-start | bytes 73736 | tf_op jit(solution)/shard_map/ppermute | solution.py:39
  103.4 8.4 %copy-start.2 = (bf16[1536,320]{0,1:T(8,128)(2,1)S(1)}, bf16[1536,320]{0,1:T(8,128)(2,1)}, u32[]{:S(2)}) copy-start(bf16[1536,320]{0,1:T(8,128)(2,1)} %param.17) | copy-start | bytes 2949124
  103.4 8.4 %copy-start.5 = (f32[1536]{0:T(1024)S(1)}, f32[1536]{0:T(1024)}, u32[]{:S(2)}) copy-start(f32[1536]{0:T(1024)} %param.15) | copy-start | bytes 18436
  110.9 0.9 copy-start.1
Sparse Core Ops, SparseCore 0:
  10.3 83.1 all-gather.2
  113.1 41.4 all-gather.4
